TPU v7x, 32 devices: a whole 2x2x4 slice. The times are simulated.
32 devices in a mesh: cores: 2 (over core), row: 4 (over y, x), vec: 4 (over z).
Axes of the slice: x: 2, y: 2, z: 4, core: 2. Of those that a mesh axis runs over, the one named last changes fastest.
Arguments:
- train_cores: float32 [4, 512, 256, 256], P('vec', 'cores', 'row'), may hold values from -0.01953125 to 0.01953125
- sketch: float32 [512, 128], P('cores'), may hold values from -6 to 6
- exit_sketch: float32 [256, 128], replicated, may hold values from -6 to 6
Outputs:
- rounded: float32 [4, 256, 256, 128], P('vec', 'cores', 'row')
- interface_bases: float32 [4, 512, 128], P('vec', 'cores')
- margins: float32 [4, 256, 512], P('vec', 'cores')
All inputs are finite; a program needn't handle non-finite values.
Results may differ from a plain program's by a relative error of at most 0.0003.
Values sent between devices are 32-bit elements; how exact they have to be, the bound alone decides.
No kernel may reach another device: no remote copies, remote signals or barrier semaphores. Data moves between devices by JAX's collectives and lax.ppermute only.
A program may use at most 192 MiB of HBM per device.

v0:
```python
import math
import jax
import jax.numpy as jnp
from jax import lax
from jax.sharding import PartitionSpec as P

MODE = 256


def broadcast(block, axis, holder):
    block = jnp.where(lax.axis_index(axis) == holder, block, jnp.zeros_like(block))
    return lax.psum(block, axis)


def product(left_mat, right_mat):
    return jnp.dot(
        left_mat, right_mat, precision=lax.Precision.HIGHEST, preferred_element_type=jnp.float32
    )


def orthonormal(gram_matrix, sketch):
    powered = product(gram_matrix, product(gram_matrix, sketch))
    chol_low = jnp.linalg.cholesky(product(powered.T, powered))
    return jax.scipy.linalg.solve_triangular(chol_low, powered.T, lower=True).T


def local(train_cores, sketch, exit_sketch):
    block_core = train_cores[0]
    full_rank = block_core.shape[0]
    mode_count = block_core.shape[1]
    kept_rank = sketch.shape[1]
    chain_len = lax.axis_size("cores")
    position = lax.axis_index("cores")
    vector_count = lax.axis_size("vec")
    identity = jnp.eye(full_rank, dtype=jnp.float32)
    zero_square = jnp.zeros((full_rank, full_rank), jnp.float32)
    row_major = block_core.reshape(full_rank * mode_count, full_rank)
    wide_core = block_core.reshape(full_rank, mode_count * full_rank)

    def forward_gram(lower_in):
        absorbed = product(lower_in.T, wide_core).reshape(full_rank * mode_count, full_rank)
        return product(absorbed.T, absorbed)

    def zero_gram(operand):
        return zero_square

    lower_prev = identity
    lower_own = identity
    gram_own = identity
    for link_index in range(chain_len):
        active = position == link_index
        partial_value = lax.cond(active, forward_gram, zero_gram, lower_prev)
        summed = jnp.where(active, lax.psum(partial_value, "row"), identity)
        factor = jnp.linalg.cholesky(summed)
        if link_index + 1 < chain_len:
            arrived = broadcast(factor, "cores", link_index)
            lower_prev = jnp.where(position == link_index + 1, arrived, lower_prev)
        lower_own = jnp.where(active, factor, lower_own)
        gram_own = jnp.where(active, summed, gram_own)
    is_last = position == chain_len - 1
    incoming = orthonormal(gram_own, exit_sketch)

    def right_map_of(incoming_frame):
        solved = jax.scipy.linalg.solve_triangular(lower_own, incoming_frame, lower=True, trans=1)
        return jnp.where(is_last, incoming_frame, solved)

    def backward_gram(incoming_frame):
        reduced = product(row_major, right_map_of(incoming_frame)).reshape(
            full_rank, mode_count * kept_rank
        )
        inner_gram = product(reduced, reduced.T)
        return product(lower_prev.T, product(inner_gram, lower_prev))

    frame_own = jnp.zeros((full_rank, kept_rank), jnp.float32)
    for link_index in range(chain_len):
        target = chain_len - 1 - link_index
        active = position == target
        partial_value = lax.cond(active, backward_gram, zero_gram, incoming)
        summed = jnp.where(active, lax.psum(partial_value, "row"), identity)
        frame = orthonormal(summed, sketch)
        if target > 0:
            arrived = broadcast(frame, "cores", target)
            incoming = jnp.where(position == target - 1, arrived, incoming)
        frame_own = jnp.where(active, frame, frame_own)
    reduced = product(row_major, right_map_of(incoming)).reshape(full_rank, mode_count * kept_rank)
    front_map = product(frame_own.T, lower_prev.T)
    shaped = product(front_map, reduced)
    rounded = (shaped * math.sqrt(kept_rank * MODE)).reshape(1, kept_rank, mode_count, kept_rank)
    bases_out = (frame_own * math.sqrt(full_rank))[None]
    gathered, frames_all = (
        lax.all_gather(shaped[None], "vec", axis=0, tiled=True),
        lax.all_gather(frame_own[None], "vec", axis=0, tiled=True),
    )
    start_env = jnp.einsum("az,qay->qzy", frame_own, frames_all, precision=lax.Precision.HIGHEST)
    mine_rows = shaped.reshape(kept_rank * mode_count, kept_rank)
    zero_env = jnp.zeros((vector_count, kept_rank, kept_rank), jnp.float32)

    def margin_terms(env_in):
        carried = jnp.einsum("qzw,qwx->qzx", env_in, gathered, precision=lax.Precision.HIGHEST)
        carried = carried.reshape(vector_count, kept_rank * mode_count, kept_rank)
        return jnp.einsum("cb,qcy->qby", mine_rows, carried, precision=lax.Precision.HIGHEST)

    def zero_margin(operand):
        return zero_env

    env_in = start_env
    env_own = zero_env
    for link_index in range(chain_len):
        active = position == link_index
        partial_value = lax.cond(active, margin_terms, zero_margin, env_in)
        summed = lax.psum(partial_value, "row")
        if link_index + 1 < chain_len:
            arrived = broadcast(summed, "cores", link_index)
            env_in = jnp.where(position == link_index + 1, arrived, env_in)
        env_own = jnp.where(active, summed, env_own)
    margins = env_own.transpose(1, 0, 2).reshape(kept_rank, vector_count * kept_rank)[None]
    return (rounded, bases_out, margins)


def solution(mesh):
    return jax.shard_map(
        local,
        mesh=mesh,
        in_specs=(P("vec", "cores", "row", None), P("cores", None), P()),
        out_specs=(
            P("vec", "cores", "row", None),
            P("vec", "cores", None),
            P("vec", "cores", None),
        ),
        check_vma=False,
    )
```

profile of v0, /device:TPU:0, one launch (start us, length us, event | category | flops | bytes accessed | tf_op | source)
XLA Modules:
  0.0 1274.4 jit_solution(12822136770054699126)
XLA Ops:
  7.3 18.5 %copy.85 = f32[32,8,64,256]{3,1,2,0:T(8,128)} copy(f32[32,8,64,256]{3,2,1,0:T(8,128)} %bitcast.211) | data formatting | bytes 33554432
  25.7 77.1 %conditional.6 = (f32[256,256]{1,0:T(8,128)S(1)}) conditional(s32[]{:T(128)} %convert_element_type.27, () %tuple.50, (f32[256,256]{0,1:T(8,128)S(1)}, f32[256,16384]{1,0:T(8,128)}) %tuple.167), branch_computations={%region_0.0_spmd, %region_1.0_spmd} | conditional | flops 25769803776 | bytes 84410376 | solution.py:52
  25.9 21.6 %fusion.102 = f32[256,16384]{1,0:T(8,128)} fusion(f32[256,256]{0,1:T(8,128)S(1)} %get-tuple-element.145, f32[256,16384]{1,0:T(8,128)} %get-tuple-element.62), kind=kOutput, calls=%fused_computation.165 | convolution fusion | flops 12884901888 | bytes 33816576 | tf_op jit(solution)/shard_map/cond/branch_1_fun/dot_general | solution.py:16
  47.5 18.0 %reshape.47 = f32[16384,256]{1,0:T(8,128)} reshape(f32[256,16384]{1,0:T(8,128)} %fusion.102) | data formatting | bytes 33554432 | tf_op jit(solution)/shard_map/cond/branch_1_fun/reshape | solution.py:41
  65.5 37.1 %fusion.103 = f32[256,256]{1,0:T(8,128)S(1)} fusion(f32[16384,256]{1,0:T(8,128)} %reshape.47), kind=kOutput, calls=%fused_computation.166 | convolution fusion | flops 12884901888 | bytes 17039360 | tf_op jit(solution)/shard_map/cond/branch_1_fun/dot_general | solution.py:16
  103.7 45.9 %all-reduce.11.cloned.1.call-done = f32[256,256]{0,1:T(8,128)} async-done(((f32[256,256]{0,1:T(8,128)}), f32[256,256]{0,1:T(8,128)}) %all-reduce.11.cloned.1.call-update) | async-done | bytes 262160 | tf_op jit(solution)/shard_map/psum | solution.py:53
  151.8 11.7 cholesky.187
  163.6 9.8 custom-call.23
  174.0 11.7 cholesky.204
  188.7 18.3 %all-reduce.13.cloned.1.call-done = f32[256,256]{0,1:T(8,128)} async-done(((f32[256,256]{0,1:T(8,128)}), f32[256,256]{0,1:T(8,128)}) %all-reduce.13.cloned.1.call-update) | async-done | bytes 262160 | tf_op jit(solution)/shard_map/psum | solution.py:12
  207.0 8.9 conditional.7
  216.9 113.5 %all-reduce.15.cloned.1.call-done = f32[256,256]{0,1:T(8,128)} async-done(((f32[256,256]{0,1:T(8,128)}), f32[256,256]{0,1:T(8,128)}) %all-reduce.15.cloned.1.call-update) | async-done | bytes 262160 | tf_op jit(solution)/shard_map/psum | solution.py:53
  330.6 11.7 cholesky.221
  342.5 9.8 custom-call.24
  352.9 11.7 cholesky.238
  366.5 11.9 cholesky.253
  379.7 9.8 custom-call.25
  392.5 8.0 conditional.8
  401.4 116.7 %all-reduce.17.cloned.1.call-done = f32[256,256]{0,1:T(8,128)} async-done(((f32[256,256]{0,1:T(8,128)}), f32[256,256]{0,1:T(8,128)}) %all-reduce.17.cloned.1.call-update) | async-done | bytes 262160 | tf_op jit(solution)/shard_map/psum | solution.py:79
  519.8 11.7 cholesky.264
  532.8 9.8 custom-call.26
  543.8 4.2 while.8
  547.9 19.7 %custom-call.28 = f32[2,128,128]{1,2,0:T(8,128)S(1)} custom-call(f32[2,128,128]{2,1,0:T(8,128)S(1)} %get-tuple-element.115), custom_call_target="InvertDiagBlocksLowerTriangular" | custom-call | tf_op jit(solution)/shard_map/jit(_solve_triangular)/triangular_solve | solution.py:64
  569.3 78.2 %conditional.9 = (f32[256,256]{0,1:T(8,128)S(1)}) conditional(s32[]{:T(128)} %convert_element_type.27, () %tuple.48, (pred[]{:T(512)}, f32[256,256]{0,1:T(8,128)S(1)}, f32[256,128]{0,1:T(8,128)S(1)}, f32[16384,256]{1,0:T(8,128)}, f32[256,256]{0,1:T(8,128)S(1)}) %tuple.166), branch_computations={%region_17.22_spmd, %region_18.23_spmd} | conditional | flops 13363265536 | bytes 71303368 | solution.py:78
  569.8 4.0 while.7
  573.8 19.7 %custom-call.22 = f32[2,128,128]{1,2,0:T(8,128)S(1)} custom-call(f32[2,128,128]{2,1,0:T(8,128)S(1)} %get-tuple-element.114), custom_call_target="InvertDiagBlocksLowerTriangular" | custom-call | tf_op jit(solution)/shard_map/cond/branch_1_fun/jit(_solve_triangular)/triangular_solve | solution.py:64
  594.2 23.1 %convolution_bitcast_fusion.2 = f32[16384,128]{0,1:T(8,128)} fusion(f32[16384,256]{1,0:T(8,128)} %get-tuple-element.80, f32[256,128]{1,0:T(8,128)S(1)} %copy.60, f32[128,128]{1,0:T(8,128)S(1)} %fusion.25, f32[128,128]{1,0:T(8,128)S(1)} %fusion.28, pred[]{:T(512)} %get-tuple-element.77), kind=kOutput, calls=%fused_computation.30 | convolution fusion | flops 6442516480 | bytes 25427968 | tf_op jit(solution)/shard_map/cond/branch_1_fun/dot_general | solution.py:16
  617.2 9.0 copy.41
  626.2 9.4 reshape.50
  635.6 10.6 fusion.109
  648.5 22.4 %convolution_bitcast_fusion.4 = f32[16384,128]{0,1:T(8,128)} fusion(f32[16384,256]{1,0:T(8,128)} %bitcast.214, f32[256,128]{0,1:T(8,128)S(1)} %broadcast_select_fusion.2, f32[128,128]{0,1:T(8,128)S(1)} %copy.64, f32[128,128]{0,1:T(8,128)S(1)} %fusion.67, pred[]{:T(512)} %eq.35), kind=kOutput, calls=%fused_computation.49 | convolution fusion | flops 6442516480 | bytes 25427968 | tf_op jit(solution)/shard_map/dot_general | solution.py:16
  670.9 9.0 copy.65
  680.0 9.8 reshape.56
  695.0 11.7 cholesky.275
  708.0 9.8 custom-call.27
  718.5 10.4 fusion.115
  728.9 4.9 reshape.58
  733.8 19.3 %all-gather = f32[1024,128]{0,1:T(8,128)S(1)} all-gather(f32[256,128]{0,1:T(8,128)S(1)} %fusion.31), channel_id=2, replica_groups=mesh['cores'=2,'row'=4,'vec'=4] {'vec'}, dimensions={0}, use_global_device_ids=true | all-gather | bytes 655360 | tf_op jit(solution)/shard_map/all_gather | solution.py:92
  753.7 264.3 %all-gather.4.cloned.1.call-done = f32[512,8192]{1,0:T(8,128)} async-done(((f32[128,8192]{1,0:T(8,128)}), f32[512,8192]{1,0:T(8,128)}) %all-gather.4.cloned.1.call-update) | async-done | bytes 16777232 | tf_op jit(solution)/shard_map/all_gather | solution.py:91
  1018.0 69.0 %conditional.10 = (f32[4,128,128]{1,2,0:T(8,128)S(1)}) conditional(s32[]{:T(128)} %convert_element_type.27, () %tuple.57, (f32[4,128,128]{1,2,0:T(8,128)S(1)}, f32[4,128,8192]{2,1,0:T(8,128)}, f32[8192,128]{1,0:T(8,128)}) %tuple.169), branch_computations={%region_20.25_spmd, %region_21.26_spmd} | conditional | flops 12884901888 | bytes 88604680 | solution.py:110
  1018.0 21.6 %fusion.106 = f32[4,128,8192]{2,1,0:T(8,128)} fusion(f32[4,128,128]{1,2,0:T(8,128)S(1)} %get-tuple-element.163, f32[4,128,8192]{2,1,0:T(8,128)} %get-tuple-element.83), kind=kOutput, calls=%fused_computation.169 | convolution fusion | flops 6442450944 | bytes 33816576 | tf_op jit(solution)/shard_map/cond/branch_1_fun/qzw,qwx->qzx/dot_general | solution.py:99
  1039.6 18.0 %reshape.51 = f32[4,8192,128]{2,1,0:T(8,128)} reshape(f32[4,128,8192]{2,1,0:T(8,128)} %fusion.106) | data formatting | bytes 33554432 | tf_op jit(solution)/shard_map/cond/branch_1_fun/reshape | solution.py:100
  1057.6 29.2 %fusion.2 = f32[4,128,128]{1,2,0:T(8,128)S(1)} fusion(f32[4,8192,128]{2,1,0:T(8,128)} %reshape.51, f32[8192,128]{1,0:T(8,128)} %get-tuple-element.84), kind=kOutput, calls=%fused_computation.2 | convolution fusion | flops 6442450944 | bytes 21233664 | tf_op jit(solution)/shard_map/cond/branch_1_fun/cb,qcy->qby/dot_general | solution.py:101
  1087.8 41.6 %all-reduce.23.cloned.1.call-done = f32[4,128,128]{1,2,0:T(8,128)} async-done(((f32[4,128,128]{1,2,0:T(8,128)}), f32[4,128,128]{1,2,0:T(8,128)}) %all-reduce.23.cloned.1.call-update) | async-done | bytes 262160 | tf_op jit(solution)/shard_map/psum | solution.py:111
  1131.9 18.6 %all-reduce.25.cloned.1.call-done = f32[4,128,128]{1,2,0:T(8,128)} async-done(((f32[4,128,128]{1,2,0:T(8,128)}), f32[4,128,128]{1,2,0:T(8,128)}) %all-reduce.25.cloned.1.call-update) | async-done | bytes 262160 | tf_op jit(solution)/shard_map/psum | solution.py:12
  1153.3 2.6 multiply_bitcast_fusion
  1155.8 2.8 copy.86
  1158.6 107.6 %all-reduce.27.cloned.1.call-done = f32[4,128,128]{1,2,0:T(8,128)} async-done(((f32[4,128,128]{1,2,0:T(8,128)}), f32[4,128,128]{1,2,0:T(8,128)}) %all-reduce.27.cloned.1.call-update) | async-done | bytes 262160 | tf_op jit(solution)/shard_map/psum | solution.py:111
  (150 shorter events, 44.2 us)
Async XLA Ops:
  7.2 510.9 %copy-start = (f32[256,128]{1,0:T(8,128)S(1)}, f32[256,128]{1,0:T(8,128)}, u32[]{:S(2)}) copy-start(f32[256,128]{1,0:T(8,128)} %param.22) | copy-start | bytes 393220
  7.2 142.4 %all-reduce.11.cloned.1.call-start = ((), (), s32[]{:S(2)}) async-start(), calls=%async_computation | async-start | bytes 524288 | tf_op jit(solution)/shard_map/psum | solution.py:53
  103.7 103.3 %all-reduce.13.cloned.1.call-start = ((), (), s32[]{:S(2)}) async-start(), calls=%async_computation.1 | async-start | bytes 524288 | tf_op jit(solution)/shard_map/psum | solution.py:12
  188.6 141.8 %all-reduce.15.cloned.1.call-start = ((), (), s32[]{:S(2)}) async-start(), calls=%async_computation.2 | async-start | bytes 524288 | tf_op jit(solution)/shard_map/psum | solution.py:53
  207.0 157.7 %copy-start.1 = (f32[256,256]{0,1:T(8,128)S(1)}, f32[256,256]{0,1:T(8,128)}, u32[]{:S(2)}) copy-start(f32[256,256]{0,1:T(8,128)} %all-reduce.11.cloned.1.call-done) | copy-start | bytes 786436
  207.0 157.7 %copy-start.8 = (f32[256,128]{1,0:T(8,128)S(1)}, f32[256,128]{1,0:T(8,128)}, u32[]{:S(2)}) copy-start(f32[256,128]{1,0:T(8,128)} %param.23) | copy-start | bytes 393220
  216.9 301.2 %all-reduce.17.cloned.1.call-start = ((), (), s32[]{:S(2)}) async-start(), calls=%async_computation.3 | async-start | bytes 524288 | tf_op jit(solution)/shard_map/psum | solution.py:79
  400.6 0.7 copy-start.4
  401.3 166.3 %all-reduce.19.cloned.1.call-start = ((), (), s32[]{:S(2)}) async-start(), calls=%async_computation.4 | async-start | bytes 262144 | tf_op jit(solution)/shard_map/psum | solution.py:12
  543.6 147.7 %all-reduce.21.cloned.1.call-start = ((), (), s32[]{:S(2)}) async-start(), calls=%async_computation.5 | async-start | bytes 524288 | tf_op jit(solution)/shard_map/psum | solution.py:79
  647.5 0.7 copy-start.5
  648.2 369.9 %all-gather.4.cloned.1.call-start = ((), (), s32[]{:S(2)}) async-start(), calls=%async_computation.9 | async-start | bytes 20971520 | tf_op jit(solution)/shard_map/all_gather | solution.py:91
  670.9 46.9 %copy-start.2 = (f32[256,128]{0,1:T(8,128)S(1)}, f32[256,128]{0,1:T(8,128)}, u32[]{:S(2)}) copy-start(f32[256,128]{0,1:T(8,128)} %fusion.32) | copy-start | bytes 393220
  728.9 400.5 %all-reduce.23.cloned.1.call-start = ((), (), s32[]{:S(2)}) async-start(), calls=%async_computation.6 | async-start | bytes 524288 | tf_op jit(solution)/shard_map/psum | solution.py:111
  1087.0 0.7 copy-start.6
  1087.8 62.8 %all-reduce.25.cloned.1.call-start = ((), (), s32[]{:S(2)}) async-start(), calls=%async_computation.7 | async-start | bytes 524288 | tf_op jit(solution)/shard_map/psum | solution.py:12
  1131.1 135.1 %all-reduce.27.cloned.1.call-start = ((), (), s32[]{:S(2)}) async-start(), calls=%async_computation.8 | async-start | bytes 524288 | tf_op jit(solution)/shard_map/psum | solution.py:111
  1152.5 0.7 copy-start.7
  1152.5 113.6 %copy-start.3 = (f32[4,128,128]{1,2,0:T(8,128)S(1)}, f32[4,128,128]{1,2,0:T(8,128)}, u32[]{:S(2)}) copy-start(f32[4,128,128]{1,2,0:T(8,128)} %all-reduce.23.cloned.1.call-done) | copy-start | bytes 786436
Sparse Core Ops, SparseCore 0:
  103.8 45.7 all-reduce.10
  188.7 18.1 all-reduce.12
  217.0 113.3 all-reduce.14
  401.4 116.5 all-reduce.16
  543.8 19.1 all-reduce.18
  648.3 43.0 all-reduce.20
  729.0 289.0 all-gather.3
  1087.9 41.4 all-reduce.22
  1132.3 18.2 all-reduce.24
  1153.9 112.2 all-reduce.26
where the time goes:
time: 1280 us; the launch traced here: 1270 us
  waiting for transfers between devices  728 us (57%)
  matrix products  189 us (15%)
  other arithmetic  185 us (14%)
  local copies, waits for them, and re-layouts  115 us (9%)
  loops' own time  20.1 us (2%)
  blocking collectives  19.3 us (2%)
  between operations  17.9 us (1%)
    psum x4, waiting for transfers between devices, local(): summed = jnp.where(active, lax.psum(partial_value, 'row'), identity)  278 us
    all_gather x1, waiting for transfers between devices, local(): lax.all_gather(shaped[None], 'vec', axis=0, tiled=True)  264 us
    psum x2, waiting for transfers between devices, local(): summed = lax.psum(partial_value, 'row')  149 us
    dot_general x18, matrix products, product(): jnp.dot(left_mat, right_mat, precision=lax.Precision.HIGHEST, preferred_e...  133 us
    another operation x13, other arithmetic, local(): factor = jnp.linalg.cholesky(summed)  68.5 us
    another operation x8, other arithmetic, right_map_of(): jax.scipy.linalg.solve_triangular(lower_own, incoming_frame, lower=True,...  39.4 us
    another operation x9, other arithmetic, orthonormal(): chol_low = jnp.linalg.cholesky(product(powered.T, powered))  37.3 us
    psum x3, waiting for transfers between devices, broadcast(): return lax.psum(block, axis)  37 us
  transfers between devices with their start and end apart: 10, of which 9 were waited for; matrix products, arithmetic and copies ran while one was open for 6% of the time, Pallas kernels for 0%

commit v1 on v0

--- a/solution.py
+++ b/solution.py
@@ -3,6 +3,7 @@
 import jax.numpy as jnp
 from jax import lax
 from jax.sharding import PartitionSpec as P
+from jax.lax import all_to_all, axis_size
 
 MODE = 256
 
@@ -87,8 +88,16 @@
     shaped = product(front_map, reduced)
     rounded = (shaped * math.sqrt(kept_rank * MODE)).reshape(1, kept_rank, mode_count, kept_rank)
     bases_out = (frame_own * math.sqrt(full_rank))[None]
+
+    def lay_knots_up(shard_in, axis_name):
+        many = axis_size(axis_name)
+        series = tuple((many if j0 == 0 else 1 for j0 in range(shard_in.ndim)))
+        back = jnp.tile(shard_in, series)
+        formed = all_to_all(back, split_axis=0, tiled=True, axis_name=axis_name, concat_axis=0)
+        return formed
+
     gathered, frames_all = (
-        lax.all_gather(shaped[None], "vec", axis=0, tiled=True),
+        lay_knots_up(shaped[None], "vec"),
         lax.all_gather(frame_own[None], "vec", axis=0, tiled=True),
     )
     start_env = jnp.einsum("az,qay->qzy", frame_own, frames_all, precision=lax.Precision.HIGHEST)

time: 1280 us -> 1390 us (1.086)
  blocking collectives: 19.3 us -> 366 us
  waiting for transfers between devices: 728 us -> 465 us
    all_gather x1, blocking collectives: 19.3 us -> 366 us  [local(): lax.all_gather(frame_own[None], 'vec', axis=0, tiled=True)]
    all_gather x1 -> x0, waiting for transfers between devices: 264 us -> none  [local(): lax.all_gather(shaped[None], 'vec', axis=0, tiled=True)]
  transfers between devices with their start and end apart: 10 -> 10, of which waited for: 9 -> 8; matrix products, arithmetic and copies ran while one was open for 6% -> 6% of each run, Pallas kernels for 0% -> 0%
where the time goes in v1:
time: 1390 us; the launch traced here: 1380 us
  waiting for transfers between devices  465 us (33%)
  blocking collectives  366 us (26%)
  other arithmetic  185 us (13%)
  matrix products  185 us (13%)
  local copies, waits for them, and re-layouts  125 us (9%)
  loops' own time  30.7 us (2%)
  between operations  17.4 us (1%)
    all_gather x1, blocking collectives, local(): lax.all_gather(frame_own[None], 'vec', axis=0, tiled=True)  366 us
    psum x4, waiting for transfers between devices, local(): summed = jnp.where(active, lax.psum(partial_value, 'row'), identity)  278 us
    psum x2, waiting for transfers between devices, local(): summed = lax.psum(partial_value, 'row')  151 us
    dot_general x18, matrix products, product(): jnp.dot(left_mat, right_mat, precision=lax.Precision.HIGHEST, preferred_e...  130 us
    another operation x13, other arithmetic, local(): factor = jnp.linalg.cholesky(summed)  68.5 us
    another operation x8, other arithmetic, right_map_of(): jax.scipy.linalg.solve_triangular(lower_own, incoming_frame, lower=True,...  39.4 us
    another operation x9, other arithmetic, orthonormal(): chol_low = jnp.linalg.cholesky(product(powered.T, powered))  37.6 us
    psum x3, waiting for transfers between devices, broadcast(): return lax.psum(block, axis)  37 us
  transfers between devices with their start and end apart: 10, of which 8 were waited for; matrix products, arithmetic and copies ran while one was open for 6% of the time, Pallas kernels for 0%

profile of v1, /device:TPU:0, one launch (start us, length us, event | category | flops | bytes accessed | tf_op | source)
XLA Modules:
  0.0 1381.9 jit_solution(12226629905804331857)
XLA Ops:
  7.3 18.5 %copy.85 = f32[32,8,64,256]{3,1,2,0:T(8,128)} copy(f32[32,8,64,256]{3,2,1,0:T(8,128)} %bitcast.210) | data formatting | bytes 33554432
  25.7 77.1 %conditional.6 = (f32[256,256]{1,0:T(8,128)S(1)}) conditional(s32[]{:T(128)} %convert_element_type.27, () %tuple.50, (f32[256,256]{0,1:T(8,128)S(1)}, f32[256,16384]{1,0:T(8,128)}) %tuple.165), branch_computations={%region_0.0_spmd, %region_1.0_spmd} | conditional | flops 25769803776 | bytes 84410376 | solution.py:53
  25.9 21.6 %fusion.102 = f32[256,16384]{1,0:T(8,128)} fusion(f32[256,256]{0,1:T(8,128)S(1)} %get-tuple-element.145, f32[256,16384]{1,0:T(8,128)} %get-tuple-element.62), kind=kOutput, calls=%fused_computation.165 | convolution fusion | flops 12884901888 | bytes 33816576 | tf_op jit(solution)/shard_map/cond/branch_1_fun/dot_general | solution.py:17
  47.5 18.0 %reshape.50 = f32[16384,256]{1,0:T(8,128)} reshape(f32[256,16384]{1,0:T(8,128)} %fusion.102) | data formatting | bytes 33554432 | tf_op jit(solution)/shard_map/cond/branch_1_fun/reshape | solution.py:42
  65.5 36.9 %fusion.103 = f32[256,256]{1,0:T(8,128)S(1)} fusion(f32[16384,256]{1,0:T(8,128)} %reshape.50), kind=kOutput, calls=%fused_computation.166 | convolution fusion | flops 12884901888 | bytes 17039360 | tf_op jit(solution)/shard_map/cond/branch_1_fun/dot_general | solution.py:17
  103.7 45.9 %all-reduce.11.cloned.1.call-done = f32[256,256]{0,1:T(8,128)} async-done(((f32[256,256]{0,1:T(8,128)}), f32[256,256]{0,1:T(8,128)}) %all-reduce.11.cloned.1.call-update) | async-done | bytes 262160 | tf_op jit(solution)/shard_map/psum | solution.py:54
  151.8 11.7 cholesky.187
  163.6 9.8 custom-call.23
  174.0 11.7 cholesky.204
  188.7 18.3 %all-reduce.13.cloned.1.call-done = f32[256,256]{0,1:T(8,128)} async-done(((f32[256,256]{0,1:T(8,128)}), f32[256,256]{0,1:T(8,128)}) %all-reduce.13.cloned.1.call-update) | async-done | bytes 262160 | tf_op jit(solution)/shard_map/psum | solution.py:13
  207.0 8.7 conditional.7
  216.7 113.6 %all-reduce.15.cloned.1.call-done = f32[256,256]{0,1:T(8,128)} async-done(((f32[256,256]{0,1:T(8,128)}), f32[256,256]{0,1:T(8,128)}) %all-reduce.15.cloned.1.call-update) | async-done | bytes 262160 | tf_op jit(solution)/shard_map/psum | solution.py:54
  330.6 11.7 cholesky.221
  342.4 9.8 custom-call.24
  352.8 11.7 cholesky.238
  366.4 12.1 cholesky.253
  379.9 9.8 custom-call.25
  392.7 7.9 conditional.8
  401.4 116.6 %all-reduce.17.cloned.1.call-done = f32[256,256]{0,1:T(8,128)} async-done(((f32[256,256]{0,1:T(8,128)}), f32[256,256]{0,1:T(8,128)}) %all-reduce.17.cloned.1.call-update) | async-done | bytes 262160 | tf_op jit(solution)/shard_map/psum | solution.py:80
  519.7 11.7 cholesky.264
  532.8 9.8 custom-call.26
  543.7 4.2 while.8
  547.9 19.7 %custom-call.28 = f32[2,128,128]{1,2,0:T(8,128)S(1)} custom-call(f32[2,128,128]{2,1,0:T(8,128)S(1)} %get-tuple-element.115), custom_call_target="InvertDiagBlocksLowerTriangular" | custom-call | tf_op jit(solution)/shard_map/jit(_solve_triangular)/triangular_solve | solution.py:65
  569.2 88.9 %conditional.9 = (f32[256,256]{0,1:T(8,128)S(1)}) conditional(s32[]{:T(128)} %convert_element_type.27, () %tuple.48, (pred[]{:T(512)}, f32[256,256]{0,1:T(8,128)S(1)}, f32[256,128]{0,1:T(8,128)S(1)}, f32[16384,256]{1,0:T(8,128)}, f32[256,256]{0,1:T(8,128)S(1)}) %tuple.164), branch_computations={%region_17.22_spmd, %region_18.23_spmd} | conditional | flops 13363265536 | bytes 71303368 | solution.py:79
  580.4 4.0 while.7
  584.4 19.7 %custom-call.22 = f32[2,128,128]{1,2,0:T(8,128)S(1)} custom-call(f32[2,128,128]{2,1,0:T(8,128)S(1)} %get-tuple-element.114), custom_call_target="InvertDiagBlocksLowerTriangular" | custom-call | tf_op jit(solution)/shard_map/cond/branch_1_fun/jit(_solve_triangular)/triangular_solve | solution.py:65
  604.8 23.1 %convolution_bitcast_fusion.2 = f32[16384,128]{0,1:T(8,128)} fusion(f32[16384,256]{1,0:T(8,128)} %get-tuple-element.80, f32[256,128]{1,0:T(8,128)S(1)} %copy.60, f32[128,128]{1,0:T(8,128)S(1)} %fusion.25, f32[128,128]{1,0:T(8,128)S(1)} %fusion.28, pred[]{:T(512)} %get-tuple-element.77), kind=kOutput, calls=%fused_computation.30 | convolution fusion | flops 6442516480 | bytes 25427968 | tf_op jit(solution)/shard_map/cond/branch_1_fun/dot_general | solution.py:17
  627.9 9.0 copy.41
  636.9 9.4 reshape.53
  646.3 10.6 fusion.109
  659.1 22.4 %convolution_bitcast_fusion.4 = f32[16384,128]{0,1:T(8,128)} fusion(f32[16384,256]{1,0:T(8,128)} %bitcast.213, f32[256,128]{0,1:T(8,128)S(1)} %broadcast_select_fusion.2, f32[128,128]{0,1:T(8,128)S(1)} %copy.64, f32[128,128]{0,1:T(8,128)S(1)} %fusion.67, pred[]{:T(512)} %eq.35), kind=kOutput, calls=%fused_computation.49 | convolution fusion | flops 6442516480 | bytes 25427968 | tf_op jit(solution)/shard_map/dot_general | solution.py:17
  681.5 9.0 copy.65
  690.6 9.8 reshape.59
  705.6 11.7 cholesky.275
  718.7 9.8 custom-call.27
  729.1 6.9 fusion.115
  738.1 7.7 tile.2
  745.8 7.0 all-to-all-start
  752.8 5.1 reshape.61
  757.9 366.0 %all-gather = f32[1024,128]{0,1:T(8,128)S(1)} all-gather(f32[256,128]{0,1:T(8,128)S(1)} %fusion.31), channel_id=2, replica_groups=mesh['cores'=2,'row'=4,'vec'=4] {'vec'}, dimensions={0}, use_global_device_ids=true | all-gather | bytes 655360 | tf_op jit(solution)/shard_map/all_gather | solution.py:101
  1124.5 69.0 %conditional.10 = (f32[4,128,128]{1,2,0:T(8,128)S(1)}) conditional(s32[]{:T(128)} %convert_element_type.27, () %tuple.57, (f32[4,128,128]{1,2,0:T(8,128)S(1)}, f32[4,128,8192]{2,1,0:T(8,128)}, f32[8192,128]{1,0:T(8,128)}) %tuple.58), branch_computations={%region_20.25_spmd, %region_21.26_spmd} | conditional | flops 12884901888 | bytes 88604680 | solution.py:119
  1124.5 21.6 %fusion.106 = f32[4,128,8192]{2,1,0:T(8,128)} fusion(f32[4,128,128]{1,2,0:T(8,128)S(1)} %get-tuple-element.163, f32[4,128,8192]{2,1,0:T(8,128)} %get-tuple-element.83), kind=kOutput, calls=%fused_computation.169 | convolution fusion | flops 6442450944 | bytes 33816576 | tf_op jit(solution)/shard_map/cond/branch_1_fun/qzw,qwx->qzx/dot_general | solution.py:108
  1146.1 18.0 %reshape.54 = f32[4,8192,128]{2,1,0:T(8,128)} reshape(f32[4,128,8192]{2,1,0:T(8,128)} %fusion.106) | data formatting | bytes 33554432 | tf_op jit(solution)/shard_map/cond/branch_1_fun/reshape | solution.py:109
  1164.1 29.2 %fusion.2 = f32[4,128,128]{1,2,0:T(8,128)S(1)} fusion(f32[4,8192,128]{2,1,0:T(8,128)} %reshape.54, f32[8192,128]{1,0:T(8,128)} %get-tuple-element.84), kind=kOutput, calls=%fused_computation.2 | convolution fusion | flops 6442450944 | bytes 21233664 | tf_op jit(solution)/shard_map/cond/branch_1_fun/cb,qcy->qby/dot_general | solution.py:110
  1194.3 43.1 %all-reduce.23.cloned.1.call-done = f32[4,128,128]{1,2,0:T(8,128)} async-done(((f32[4,128,128]{1,2,0:T(8,128)}), f32[4,128,128]{1,2,0:T(8,128)}) %all-reduce.23.cloned.1.call-update) | async-done | bytes 262160 | tf_op jit(solution)/shard_map/psum | solution.py:120
  1239.9 18.6 %all-reduce.25.cloned.1.call-done = f32[4,128,128]{1,2,0:T(8,128)} async-done(((f32[4,128,128]{1,2,0:T(8,128)}), f32[4,128,128]{1,2,0:T(8,128)}) %all-reduce.25.cloned.1.call-update) | async-done | bytes 262160 | tf_op jit(solution)/shard_map/psum | solution.py:13
  1263.8 2.8 copy.86
  1266.6 107.6 %all-reduce.27.cloned.1.call-done = f32[4,128,128]{1,2,0:T(8,128)} async-done(((f32[4,128,128]{1,2,0:T(8,128)}), f32[4,128,128]{1,2,0:T(8,128)}) %all-reduce.27.cloned.1.call-update) | async-done | bytes 262160 | tf_op jit(solution)/shard_map/psum | solution.py:120
  (152 shorter events, 48.8 us)
Async XLA Ops:
  7.2 510.8 %copy-start = (f32[256,128]{1,0:T(8,128)S(1)}, f32[256,128]{1,0:T(8,128)}, u32[]{:S(2)}) copy-start(f32[256,128]{1,0:T(8,128)} %param.22) | copy-start | bytes 393220
  7.2 142.4 %all-reduce.11.cloned.1.call-start = ((), (), s32[]{:S(2)}) async-start(), calls=%async_computation.1 | async-start | bytes 524288 | tf_op jit(solution)/shard_map/psum | solution.py:54
  103.7 103.3 %all-reduce.13.cloned.1.call-start = ((), (), s32[]{:S(2)}) async-start(), calls=%async_computation.2 | async-start | bytes 524288 | tf_op jit(solution)/shard_map/psum | solution.py:13
  188.6 141.7 %all-reduce.15.cloned.1.call-start = ((), (), s32[]{:S(2)}) async-start(), calls=%async_computation.3 | async-start | bytes 524288 | tf_op jit(solution)/shard_map/psum | solution.py:54
  207.0 157.7 %copy-start.2 = (f32[256,256]{0,1:T(8,128)S(1)}, f32[256,256]{0,1:T(8,128)}, u32[]{:S(2)}) copy-start(f32[256,256]{0,1:T(8,128)} %all-reduce.11.cloned.1.call-done) | copy-start | bytes 786436
  207.0 157.7 %copy-start.9 = (f32[256,128]{1,0:T(8,128)S(1)}, f32[256,128]{1,0:T(8,128)}, u32[]{:S(2)}) copy-start(f32[256,128]{1,0:T(8,128)} %param.23) | copy-start | bytes 393220
  216.7 301.3 %all-reduce.17.cloned.1.call-start = ((), (), s32[]{:S(2)}) async-start(), calls=%async_computation.4 | async-start | bytes 524288 | tf_op jit(solution)/shard_map/psum | solution.py:80
  400.6 0.7 copy-start.5
  401.3 166.2 %all-reduce.19.cloned.1.call-start = ((), (), s32[]{:S(2)}) async-start(), calls=%async_computation.5 | async-start | bytes 262144 | tf_op jit(solution)/shard_map/psum | solution.py:13
  543.6 158.4 %all-reduce.21.cloned.1.call-start = ((), (), s32[]{:S(2)}) async-start(), calls=%async_computation.6 | async-start | bytes 524288 | tf_op jit(solution)/shard_map/psum | solution.py:80
  658.1 0.7 copy-start.6
  681.5 47.0 %copy-start.3 = (f32[256,128]{0,1:T(8,128)S(1)}, f32[256,128]{0,1:T(8,128)}, u32[]{:S(2)}) copy-start(f32[256,128]{0,1:T(8,128)} %fusion.32) | copy-start | bytes 393220
  736.0 2.0 copy-start.1
  745.8 378.7 %all-to-all-start = ((f32[4,128,8192]{2,1,0:T(8,128)}), f32[4,128,8192]{2,1,0:T(8,128)}, u32[]{:S(2)}, u32[]{:S(2)}) async-start(f32[4,128,8192]{2,1,0:T(8,128)} %tile.2), calls=%async_computation | async-start | bytes 33554432 | tf_op jit(solution)/shard_map/all_to_all | solution.py:96
  752.8 484.6 %all-reduce.23.cloned.1.call-start = ((), (), s32[]{:S(2)}) async-start(), calls=%async_computation.7 | async-start | bytes 524288 | tf_op jit(solution)/shard_map/psum | solution.py:120
  1193.5 0.7 copy-start.7
  1194.3 64.3 %all-reduce.25.cloned.1.call-start = ((), (), s32[]{:S(2)}) async-start(), calls=%async_computation.8 | async-start | bytes 524288 | tf_op jit(solution)/shard_map/psum | solution.py:13
  1239.1 135.1 %all-reduce.27.cloned.1.call-start = ((), (), s32[]{:S(2)}) async-start(), calls=%async_computation.9 | async-start | bytes 524288 | tf_op jit(solution)/shard_map/psum | solution.py:120
  1260.5 0.7 copy-start.8
  1260.6 113.6 %copy-start.4 = (f32[4,128,128]{1,2,0:T(8,128)S(1)}, f32[4,128,128]{1,2,0:T(8,128)}, u32[]{:S(2)}) copy-start(f32[4,128,128]{1,2,0:T(8,128)} %all-reduce.23.cloned.1.call-done) | copy-start | bytes 786436
Sparse Core Ops, SparseCore 0:
  103.8 45.7 all-reduce.10
  188.7 18.2 all-reduce.12
  216.8 113.5 all-reduce.14
  401.5 116.4 all-reduce.16
  543.7 18.9 all-reduce.18
  658.9 43.0 all-reduce.20
  1194.4 42.9 all-reduce.22
  1240.3 18.2 all-reduce.24
  1262.0 112.0 all-reduce.26
